TPU v7x, 512 devices: a whole 4x4x16 slice. The times are simulated.
512 devices in a mesh: dp: 8 (over z_hi, y), shard: 64 (over x, z_lo, core).
Axes of the slice: x: 4, y: 4, z: 16 (z_hi: 2, z_lo: 8; z = z_hi * 8 + z_lo), core: 2. Of those that a mesh axis runs over, the one named last changes fastest.
Arguments:
- context: bfloat16 [8192, 4096], P('shard'), may hold values from -16 to 16
- projected: bfloat16 [8192, 4096], P('shard', 'dp'), may hold values from -6 to 6
- cotangent: bfloat16 [8192, 4096], P('shard', 'dp'), may hold values from -16 to 16
- modality: int32 [8192], P('shard'), may hold values from 0 to 2
- out_weight: bfloat16 [4096, 3, 4096], P('shard', None, 'dp'), may hold values from -0.09375 to 0.09375
- out_gain: float32 [3, 4096], P(None, 'dp'), may hold values from 0.25 to 1.75
Outputs:
- grad_context: bfloat16 [8192, 4096], P('shard', 'dp')
- grad_weight: float32 [4096, 3, 4096], P('shard', None, 'dp')
- grad_gain: float32 [3, 4096], P(None, 'dp')
All inputs are finite; a program needn't handle non-finite values.
Results may differ from a plain program's by a relative error of at most 0.0049.
Values may be sent and summed in bfloat16 or wider, within the bound.
No kernel may reach another device: no remote copies, remote signals or barrier semaphores. Data moves between devices by JAX's collectives and lax.ppermute only.
A program may use at most 64 MiB of HBM per device.

v0:
```python
import jax
import jax.numpy as jnp
from jax import lax
from jax.sharding import Mesh
from jax.sharding import PartitionSpec as P

D = 4096
DP = ("dp_0", "dp_1")
EPS = 1e-06


def from_everyone(shard, axis):
    count = lax.axis_size(axis)
    return lax.all_to_all(
        jnp.broadcast_to(shard[None], (count, *shard.shape)), axis, 0, 0, tiled=True
    )


def of_everyone(shard, axis):
    everything = from_everyone(shard, axis)
    return jnp.sum(everything, axis=0)


def packed_total(arrays, axis):
    ravelled, at, outs = (jnp.concatenate([a.reshape(-1) for a in arrays]), 0, [])
    total = of_everyone(ravelled, axis)
    for a in arrays:
        outs.append(total[at : at + a.size].reshape(a.shape))
        at += a.size
    return tuple(outs)


def sum_in_order(pieces, axes, order):
    lengths = [lax.axis_size(a) for a in axes]
    pieces = pieces.reshape(*lengths, *pieces.shape[1:])
    pieces = pieces.transpose(*order, *range(len(axes), pieces.ndim))
    pieces = pieces.reshape(-1, *pieces.shape[len(axes) :])
    for k in order:
        pieces = lax.psum_scatter(pieces, axes[k], scatter_dimension=0, tiled=True)
    return pieces[0]


def cut_along(shard, dim, count):
    lengths = shard.shape
    pieces = shard.reshape(*lengths[:dim], count, lengths[dim] // count, *lengths[dim + 1 :])
    return jnp.moveaxis(pieces, dim, 0)


def summed_rows(shard, axes, order, dim):
    count = lax.axis_size(axes)
    return sum_in_order(cut_along(shard, dim, count), axes, order)


def local(context, projected, cotangent, modality, out_weight, out_gain):
    towers = out_weight.shape[1]
    tower_ids = jnp.arange(towers, dtype=jnp.int32)
    onehot = (modality[:, None] == tower_ids[None, :]).astype(jnp.float32)
    proj_float = projected.astype(jnp.float32)
    cot_float = cotangent.astype(jnp.float32)
    gain_tok = jnp.dot(onehot, out_gain, precision=lax.Precision.HIGHEST)
    scaled = cot_float * gain_tok
    squares, raw_inner = packed_total(
        (
            jnp.sum(proj_float * proj_float, axis=1, keepdims=True),
            jnp.sum(scaled * proj_float, axis=1, keepdims=True),
        ),
        DP,
    )
    inverse_rms = lax.rsqrt(squares / D + EPS)
    normed = proj_float * inverse_rms
    inner = inverse_rms * raw_inner
    gain_terms = jnp.dot(onehot.T, cot_float * normed, precision=lax.Precision.HIGHEST)
    grad_gain = of_everyone(gain_terms, "shard")
    grad_proj = (inverse_rms * (scaled - normed * (inner / D))).astype(jnp.bfloat16)
    column_rows = lax.all_to_all(context, "shard", split_axis=1, concat_axis=0, tiled=True)
    row_count = out_weight.shape[0]
    piece_grad = lax.all_gather(grad_proj, "shard", axis=0, tiled=True)
    piece_ids = lax.all_gather(modality, "shard", axis=0, tiled=True)
    count = piece_grad.shape[0]
    piece_partial = jnp.zeros((count, row_count), jnp.float32)
    updated = []
    for member in range(towers):
        chosen = piece_ids[:, None] == member
        product = lax.dot_general(
            piece_grad,
            out_weight[:, member, :],
            (((1,), (1,)), ((), ())),
            preferred_element_type=jnp.float32,
        )
        piece_partial = piece_partial + chosen.astype(jnp.float32) * product
        masked = jnp.where(chosen, column_rows, jnp.zeros_like(column_rows))
        updated.append(
            lax.dot_general(
                masked, piece_grad, (((0,), (0,)), ((), ())), preferred_element_type=jnp.float32
            )
        )
    partial_value = piece_partial
    weight_accs, partial_value = (tuple(updated), partial_value)
    grad_weight = jnp.stack(weight_accs, axis=1)
    shard_count = lax.axis_size("shard")
    replica_count = lax.axis_size(DP)
    tok_here = grad_proj.shape[0]
    sub_rows = tok_here // replica_count
    grouped = partial_value.reshape(shard_count, replica_count, sub_rows, row_count)
    reduced = summed_rows(grouped, DP, (1, 0), 1).astype(jnp.bfloat16)
    reduced = reduced.reshape(shard_count, sub_rows, row_count)
    spread = lax.all_to_all(reduced, "shard", split_axis=0, concat_axis=2, tiled=True)
    settled = lax.all_to_all(spread, DP, split_axis=2, concat_axis=1, tiled=True)
    grad_context = settled.reshape(tok_here, settled.shape[2])
    return (grad_context, grad_weight, grad_gain)


def solution(mesh):
    finer = Mesh(mesh.devices.reshape(2, 4, mesh.shape["shard"]), ("dp_0", "dp_1", "shard"))
    return jax.shard_map(
        local,
        mesh=finer,
        in_specs=(
            P("shard", None),
            P("shard", DP),
            P("shard", DP),
            P("shard"),
            P("shard", None, DP),
            P(None, DP),
        ),
        out_specs=(P("shard", DP), P("shard", None, DP), P(None, DP)),
        check_vma=False,
    )
```

profile of v0, /device:TPU:32, one launch (start us, length us, event | category | flops | bytes accessed | tf_op | source)
XLA Modules:
  0.0 406.7 jit_solution(18081353275957798756)
XLA Ops:
  7.2 0.0 all-gather.3.cloned.1.call-start
  7.2 0.6 copy-done
  7.9 1.4 fusion.16
  9.3 31.5 %all_to_all.63 = f32[8,1,256]{2,1,0:T(1,128)S(1)} all-to-all(f32[8,1,256]{2,1,0:T(1,128)S(1)} %broadcast_in_dim.35), channel_id=1, replica_groups=mesh['dp_0'=2,'dp_1'=4,'shard'=64] {'dp_0','dp_1'}, dimensions={0} | all-to-all | bytes 16384 | tf_op jit(solution)/shard_map/all_to_all | solution.py:14
  40.9 1.7 fusion.14
  42.6 0.0 all-gather.3.cloned.1.call-update
  42.6 113.4 %all-gather = s32[64,1,128]{2,1,0:T(1,128)S(1)} all-gather(s32[1,1,128]{2,1,0:T(1,128)} %bitcast.89), channel_id=1, replica_groups=mesh['dp_0'=2,'dp_1'=4,'shard'=64] {'shard'}, dimensions={0}, use_global_device_ids=true | all-gather | bytes 33280 | tf_op jit(solution)/shard_map/all_gather | solution.py:78
  156.0 1.3 fusion.15
  157.3 0.9 broadcast_in_dim.39
  158.2 10.1 %all-to-all-start.4 = ((f32[64,3,512]{2,1,0:T(4,128)}), f32[64,3,512]{2,1,0:T(4,128)S(1)}, u32[]{:S(2)}, u32[]{:S(2)}) async-start(f32[64,3,512]{2,1,0:T(4,128)} %broadcast_in_dim.39), calls=%async_computation.6 | async-start | bytes 1048576 | tf_op jit(solution)/shard_map/all_to_all | solution.py:14
  168.2 0.0 reduce-scatter.3.cloned.1.call-start
  168.3 0.0 all-gather.3.cloned.1.call-done
  168.3 6.2 %convolution_multiply_fusion = f32[8192,64]{0,1:T(8,128)S(1)} fusion(bf16[8192,512]{1,0:T(8,128)(2,1)} %all-gather.3.cloned.1.call-done, f32[8192]{0:T(1024)S(1)} %get-tuple-element.11, bf16[64,3,512]{2,0,1:T(8,128)(2,1)} %param.10), kind=kOutput, calls=%fused_computation | convolution fusion | flops 537395200 | bytes 10584064 | tf_op jit(solution)/shard_map/dot_general | solution.py:84
  174.5 2.6 convolution_multiply_fusion.1
  177.2 2.6 fusion.1
  179.8 2.7 copy.46
  182.5 4.5 %copy.47 = f32[2,4,64,1,16,64]{5,4,2,0,1,3:T(8,128)} copy(f32[2,4,64,1,16,64]{5,4,1,0,2,3:T(8,128)} %bitcast.81) | data formatting | bytes 4194304 | tf_op jit(solution)/shard_map/reshape | solution.py:35
  187.0 0.0 reduce-scatter.3.cloned.1.call-update
  187.1 1.2 copy-done.2
  188.3 1.3 copy.52
  189.5 6.7 %all-to-all-done.4 = f32[64,3,512]{2,1,0:T(4,128)S(1)} async-done(((f32[64,3,512]{2,1,0:T(4,128)}), f32[64,3,512]{2,1,0:T(4,128)S(1)}, u32[]{:S(2)}, u32[]{:S(2)}) %all-to-all-start.4) | async-done | bytes 393248 | tf_op jit(solution)/shard_map/all_to_all | solution.py:14
  196.3 9.1 %all-to-all-start.3 = ((bf16[128,64,64]{0,2,1:T(8,128)(2,1)}), bf16[128,64,64]{0,2,1:T(8,128)(2,1)S(1)}, u32[]{:S(2)}, u32[]{:S(2)}) async-start(bf16[128,64,64]{0,2,1:T(8,128)(2,1)} %bitcast.20), calls=%async_computation.5 | async-start | bytes 2097152 | tf_op jit(solution)/shard_map/all_to_all | solution.py:75
  205.4 0.0 reduce-scatter.5.cloned.1.call-start
  205.5 33.3 %reduce-scatter.3.cloned.1.call-done = f32[2,64,1,16,64]{4,3,1,0,2:T(8,128)} async-done(((f32[8,64,1,16,64]{4,3,1,0,2:T(8,128)}), f32[2,64,1,16,64]{4,3,1,0,2:T(8,128)}) %reduce-scatter.3.cloned.1.call-update) | async-done | bytes 524304 | tf_op jit(solution)/shard_map/reduce_scatter | solution.py:39
  238.8 0.0 reduce-scatter.5.cloned.1.call-update
  238.8 0.7 reduce_sum.39
  239.5 15.5 %all-to-all-done.3 = bf16[128,64,64]{0,2,1:T(8,128)(2,1)S(1)} async-done(((bf16[128,64,64]{0,2,1:T(8,128)(2,1)}), bf16[128,64,64]{0,2,1:T(8,128)(2,1)S(1)}, u32[]{:S(2)}, u32[]{:S(2)}) %all-to-all-start.3) | async-done | bytes 1048608 | tf_op jit(solution)/shard_map/all_to_all | solution.py:75
  255.1 5.3 %convolution_bitcast_fusion = f32[64,1,512]{2,0,1:T(8,128)S(1)} fusion(bf16[8192,512]{1,0:T(8,128)(2,1)} %all-gather.3.cloned.1.call-done, pred[8192]{0:T(1024)(128)(4,1)S(1)} %get-tuple-element.12, bf16[128,64,64]{0,2,1:T(8,128)(2,1)S(1)} %all-to-all-done.3), kind=kOutput, calls=%fused_computation.6 | convolution fusion | flops 537395200 | bytes 9576448 | tf_op jit(solution)/shard_map/dot_general | solution.py:93
  260.3 46.1 %reduce-scatter.5.cloned.1.call-done = f32[1,64,1,16,64]{4,3,1,0,2:T(8,128)} async-done(((f32[2,64,1,16,64]{4,3,1,0,2:T(8,128)}), f32[1,64,1,16,64]{4,3,1,0,2:T(8,128)}) %reduce-scatter.5.cloned.1.call-update) | async-done | bytes 262160 | tf_op jit(solution)/shard_map/reduce_scatter | solution.py:39
  306.4 1.1 convert_bitcast_fusion
  307.5 0.9 reshape.65
  308.3 14.9 %all-to-all-start.1 = ((bf16[64,2,512]{2,1,0:T(2,128)(2,1)}), bf16[64,2,512]{2,1,0:T(2,128)(2,1)S(1)}, u32[]{:S(2)}, u32[]{:S(2)}) async-start(bf16[64,2,512]{2,1,0:T(2,128)(2,1)} %reshape.65), calls=%async_computation.3 | async-start | bytes 262144 | tf_op jit(solution)/shard_map/all_to_all | solution.py:107
  323.2 4.9 %convolution_bitcast_fusion.1 = f32[64,1,512]{2,0,1:T(8,128)S(1)} fusion(bf16[8192,512]{1,0:T(8,128)(2,1)} %all-gather.3.cloned.1.call-done, pred[8192]{0:T(1024)(128)(4,1)S(1)} %get-tuple-element.14, bf16[128,64,64]{0,2,1:T(8,128)(2,1)S(1)} %all-to-all-done.3), kind=kOutput, calls=%fused_computation.7 | convolution fusion | flops 537395200 | bytes 9576448 | tf_op jit(solution)/shard_map/dot_general | solution.py:93
  328.1 8.7 %all-to-all-done.1 = bf16[64,2,512]{2,1,0:T(2,128)(2,1)S(1)} async-done(((bf16[64,2,512]{2,1,0:T(2,128)(2,1)}), bf16[64,2,512]{2,1,0:T(2,128)(2,1)S(1)}, u32[]{:S(2)}, u32[]{:S(2)}) %all-to-all-start.1) | async-done | bytes 131104 | tf_op jit(solution)/shard_map/all_to_all | solution.py:107
  336.9 0.2 reshape.66
  337.1 0.1 copy.48
  337.2 0.3 all_to_all.49
  337.4 2.7 copy.49
  340.2 0.5 broadcast.57
  340.7 23.5 %reduce.1 = bf16[4096,16]{1,0:T(8,128)(2,1)} reduce(bf16[4096,1,16]{2,1,0:T(2,128)(2,1)S(1)} %bitcast.82, bf16[]{:T(256)} %broadcast.57), dimensions={1}, to_apply=%bitcast.58.reduce_sub_computation | reduce | bytes 262146
  364.2 3.1 reshape.67
  367.3 10.1 %all-to-all-start.2 = ((bf16[8,2,4096]{2,1,0:T(2,128)(2,1)}), bf16[8,2,4096]{2,1,0:T(2,128)(2,1)S(1)}, u32[]{:S(2)}, u32[]{:S(2)}) async-start(bf16[8,2,4096]{2,1,0:T(2,128)(2,1)} %reshape.67), calls=%async_computation.4 | async-start | bytes 262144 | tf_op jit(solution)/shard_map/all_to_all | solution.py:108
  377.3 4.9 %convolution_bitcast_fusion.2 = f32[64,1,512]{2,0,1:T(8,128)S(1)} fusion(bf16[8192,512]{1,0:T(8,128)(2,1)} %all-gather.3.cloned.1.call-done, pred[8192]{0:T(1024)(128)(4,1)S(1)} %get-tuple-element.6, bf16[128,64,64]{0,2,1:T(8,128)(2,1)S(1)} %all-to-all-done.3), kind=kOutput, calls=%fused_computation.8 | convolution fusion | flops 537395200 | bytes 9576448 | tf_op jit(solution)/shard_map/dot_general | solution.py:93
  382.3 0.8 pad_maximum_fusion
  383.0 12.6 %all-to-all-done.2 = bf16[8,2,4096]{2,1,0:T(2,128)(2,1)S(1)} async-done(((bf16[8,2,4096]{2,1,0:T(2,128)(2,1)}), bf16[8,2,4096]{2,1,0:T(2,128)(2,1)S(1)}, u32[]{:S(2)}, u32[]{:S(2)}) %all-to-all-start.2) | async-done | bytes 131104 | tf_op jit(solution)/shard_map/all_to_all | solution.py:108
  395.6 1.8 reshape.68
  397.4 2.0 copy.50
  399.5 0.7 copy.51
  (13 shorter events, 0.1 us)
Async XLA Ops:
  7.2 0.7 copy-start
  7.2 161.1 %all-gather.3.cloned.1.call-start = ((), (), s32[]{:S(2)}) async-start(), calls=%async_computation.7 | async-start | bytes 8519680 | tf_op jit(solution)/shard_map/all_gather | solution.py:77
  158.2 38.1 %all-to-all-start.4 = ((f32[64,3,512]{2,1,0:T(4,128)}), f32[64,3,512]{2,1,0:T(4,128)S(1)}, u32[]{:S(2)}, u32[]{:S(2)}) async-start(f32[64,3,512]{2,1,0:T(4,128)} %broadcast_in_dim.39), calls=%async_computation.6 | async-start | bytes 1048576 | tf_op jit(solution)/shard_map/all_to_all | solution.py:14
  168.2 70.5 %reduce-scatter.3.cloned.1.call-start = ((), (), s32[]{:S(2)}) async-start(), calls=%async_computation.8 | async-start | bytes 5242880 | tf_op jit(solution)/shard_map/reduce_scatter | solution.py:39
  168.3 6.2 %copy-start.1 = (bf16[8192,512]{1,0:T(8,128)(2,1)S(1)}, bf16[8192,512]{1,0:T(8,128)(2,1)}, u32[]{:S(2)}) copy-start(bf16[8192,512]{1,0:T(8,128)(2,1)} %all-gather.3.cloned.1.call-done) | copy-start | bytes 25165828
  168.3 6.2 %copy-start.3 = (bf16[64,3,512]{2,0,1:T(8,128)(2,1)S(1)}, bf16[64,3,512]{2,0,1:T(8,128)(2,1)}, u32[]{:S(2)}) copy-start(bf16[64,3,512]{2,0,1:T(8,128)(2,1)} %param.10) | copy-start | bytes 589828
  187.0 1.2 copy-start.2
  196.3 58.8 %all-to-all-start.3 = ((bf16[128,64,64]{0,2,1:T(8,128)(2,1)}), bf16[128,64,64]{0,2,1:T(8,128)(2,1)S(1)}, u32[]{:S(2)}, u32[]{:S(2)}) async-start(bf16[128,64,64]{0,2,1:T(8,128)(2,1)} %bitcast.20), calls=%async_computation.5 | async-start | bytes 2097152 | tf_op jit(solution)/shard_map/all_to_all | solution.py:75
  205.4 101.0 %reduce-scatter.5.cloned.1.call-start = ((), (), s32[]{:S(2)}) async-start(), calls=%async_computation.9 | async-start | bytes 1572864 | tf_op jit(solution)/shard_map/reduce_scatter | solution.py:39
  308.3 28.5 %all-to-all-start.1 = ((bf16[64,2,512]{2,1,0:T(2,128)(2,1)}), bf16[64,2,512]{2,1,0:T(2,128)(2,1)S(1)}, u32[]{:S(2)}, u32[]{:S(2)}) async-start(bf16[64,2,512]{2,1,0:T(2,128)(2,1)} %reshape.65), calls=%async_computation.3 | async-start | bytes 262144 | tf_op jit(solution)/shard_map/all_to_all | solution.py:107
  367.3 28.3 %all-to-all-start.2 = ((bf16[8,2,4096]{2,1,0:T(2,128)(2,1)}), bf16[8,2,4096]{2,1,0:T(2,128)(2,1)S(1)}, u32[]{:S(2)}, u32[]{:S(2)}) async-start(bf16[8,2,4096]{2,1,0:T(2,128)(2,1)} %reshape.67), calls=%async_computation.4 | async-start | bytes 262144 | tf_op jit(solution)/shard_map/all_to_all | solution.py:108
Sparse Core Ops, SparseCore 0:
  42.7 119.8 all-gather.2
  187.2 51.5 reduce-scatter.2
  241.6 64.7 reduce-scatter.4
where the time goes:
time: 408 us; the launch traced here: 407 us
  blocking collectives  145 us (36%)
  waiting for transfers between devices  123 us (30%)
  starting transfers between devices  44.3 us (11%)
  matrix products  29.2 us (7%)
  other arithmetic  27.8 us (7%)
  local copies, waits for them, and re-layouts  23.6 us (6%)
  between operations  13.9 us (3%)
    all_gather x1, blocking collectives, local(): piece_ids = lax.all_gather(modality, 'shard', axis=0, tiled=True)  113 us
    reduce_scatter x2, waiting for transfers between devices, sum_in_order(): pieces = lax.psum_scatter(pieces, axes[k], scatter_dimension=0, tiled=True)  79.4 us
    all_to_all x1, blocking collectives, from_everyone(): lax.all_to_all(jnp.broadcast_to(shard[None], (count, *shard.shape)), axis...  31.5 us
    unnamed x1, other arithmetic  23.5 us
    all_to_all x1, waiting for transfers between devices, local(): lax.all_to_all(context, 'shard', split_axis=1, concat_axis=0, tiled=True)  15.5 us
    dot_general x3, matrix products, local(): lax.dot_general(masked, piece_grad, (((0,), (0,)), ((), ())), preferred_e...  15.1 us
    all_to_all x1, starting transfers between devices, local(): lax.all_to_all(reduced, 'shard', split_axis=0, concat_axis=2, tiled=True)  14.9 us
    all_to_all x1, waiting for transfers between devices, local(): lax.all_to_all(spread, DP, split_axis=2, concat_axis=1, tiled=True)  12.6 us
  transfers between devices with their start and end apart: 7, of which 6 were waited for; matrix products, arithmetic and copies ran while one was open for 10% of the time, Pallas kernels for 0%

commit v1 on v0

--- a/solution.py
+++ b/solution.py
@@ -75,7 +75,15 @@
     column_rows = lax.all_to_all(context, "shard", split_axis=1, concat_axis=0, tiled=True)
     row_count = out_weight.shape[0]
     piece_grad = lax.all_gather(grad_proj, "shard", axis=0, tiled=True)
-    piece_ids = lax.all_gather(modality, "shard", axis=0, tiled=True)
+    piece_ids = jnp.concatenate(
+        lax.all_to_all(
+            jnp.stack([modality for _ in range(lax.axis_size("shard"))], axis=0),
+            "shard",
+            split_axis=0,
+            concat_axis=0,
+        ),
+        0,
+    )
     count = piece_grad.shape[0]
     piece_partial = jnp.zeros((count, row_count), jnp.float32)
     updated = []

time: 408 us -> 416 us (1.020)
  waiting for transfers between devices: 123 us -> 240 us
  blocking collectives: 145 us -> 31.5 us
  starting transfers between devices: 44.3 us -> 48.6 us
    all_gather x1 -> x0, blocking collectives: 113 us -> none  [local(): piece_ids = lax.all_gather(modality, 'shard', axis=0, tiled=True)]
    all_gather x1, waiting for transfers between devices: 0.02 us -> 106 us  [local(): piece_grad = lax.all_gather(grad_proj, 'shard', axis=0, tiled=True)]
    reduce_scatter x2, waiting for transfers between devices: 79.4 us -> 93.6 us  [sum_in_order(): pieces = lax.psum_scatter(pieces, axes[k], scatter_dimension=0, tiled=True)]
    all_to_all x0 -> x1, waiting for transfers between devices: none -> 10.2 us  [local(): lax.all_to_all(jnp.stack([modality for _ in range(lax.axis_size('shard'))...]
    all_to_all x0 -> x1, starting transfers between devices: none -> 9.05 us  [local(): lax.all_to_all(jnp.stack([modality for _ in range(lax.axis_size('shard'))...]
    all_to_all x1, waiting for transfers between devices: 15.5 us -> 8.62 us  [local(): lax.all_to_all(context, 'shard', split_axis=1, concat_axis=0, tiled=True)]
    all_to_all x1, waiting for transfers between devices: 6.73 us -> 0.01 us  [from_everyone(): lax.all_to_all(jnp.broadcast_to(shard[None], (count, *shard.shape)), axis...]
    all_to_all x1, starting transfers between devices: 10.1 us -> 5.43 us  [from_everyone(): lax.all_to_all(jnp.broadcast_to(shard[None], (count, *shard.shape)), axis...]
  transfers between devices with their start and end apart: 7 -> 8, of which waited for: 6 -> 7; matrix products, arithmetic and copies ran while one was open for 10% -> 10% of each run, Pallas kernels for 0% -> 0%
where the time goes in v1:
time: 416 us; the launch traced here: 415 us
  waiting for transfers between devices  240 us (58%)
  starting transfers between devices  48.6 us (12%)
  blocking collectives  31.5 us (8%)
  matrix products  28.9 us (7%)
  other arithmetic  27.8 us (7%)
  local copies, waits for them, and re-layouts  24.9 us (6%)
  between operations  13.9 us (3%)
    all_gather x1, waiting for transfers between devices, local(): piece_grad = lax.all_gather(grad_proj, 'shard', axis=0, tiled=True)  106 us
    reduce_scatter x2, waiting for transfers between devices, sum_in_order(): pieces = lax.psum_scatter(pieces, axes[k], scatter_dimension=0, tiled=True)  93.6 us
    all_to_all x1, blocking collectives, from_everyone(): lax.all_to_all(jnp.broadcast_to(shard[None], (count, *shard.shape)), axis...  31.5 us
    unnamed x1, other arithmetic  23.5 us
    all_to_all x1, starting transfers between devices, local(): lax.all_to_all(reduced, 'shard', split_axis=0, concat_axis=2, tiled=True)  15.1 us
    dot_general x3, matrix products, local(): lax.dot_general(masked, piece_grad, (((0,), (0,)), ((), ())), preferred_e...  14.8 us
    all_to_all x1, waiting for transfers between devices, local(): lax.all_to_all(spread, DP, split_axis=2, concat_axis=1, tiled=True)  12.6 us
    dot_general x3, matrix products, local(): lax.dot_general(piece_grad, out_weight[:, member, :], (((1,), (1,)), ((),...  11.4 us
  transfers between devices with their start and end apart: 8, of which 7 were waited for; matrix products, arithmetic and copies ran while one was open for 10% of the time, Pallas kernels for 0%

profile of v1, /device:TPU:32, one launch (start us, length us, event | category | flops | bytes accessed | tf_op | source)
XLA Modules:
  0.0 415.4 jit_solution(859353458539311078)
XLA Ops:
  7.2 0.0 all-gather.2.cloned.1.call-start
  7.2 0.6 copy-done
  7.9 1.4 fusion.16
  9.3 31.5 %all_to_all.69 = f32[8,1,256]{2,1,0:T(1,128)S(1)} all-to-all(f32[8,1,256]{2,1,0:T(1,128)S(1)} %broadcast_in_dim.32), channel_id=1, replica_groups=mesh['dp_0'=2,'dp_1'=4,'shard'=64] {'dp_0','dp_1'}, dimensions={0} | all-to-all | bytes 16384 | tf_op jit(solution)/shard_map/all_to_all | solution.py:14
  40.9 1.7 fusion.14
  42.6 1.3 stack.10
  43.9 9.0 %all-to-all-start = ((s32[64,1,128]{2,1,0:T(1,128)}), s32[64,1,128]{2,1,0:T(1,128)S(1)}, u32[]{:S(2)}, u32[]{:S(2)}) async-start(s32[64,1,128]{2,1,0:T(1,128)} %stack.10), calls=%async_computation | async-start | bytes 65536 | tf_op jit(solution)/shard_map/all_to_all | solution.py:79
  52.9 1.3 fusion.15
  54.2 10.2 %all-to-all-done = s32[64,1,128]{2,1,0:T(1,128)S(1)} async-done(((s32[64,1,128]{2,1,0:T(1,128)}), s32[64,1,128]{2,1,0:T(1,128)S(1)}, u32[]{:S(2)}, u32[]{:S(2)}) %all-to-all-start) | async-done | bytes 32800 | tf_op jit(solution)/shard_map/all_to_all | solution.py:79
  64.4 0.9 broadcast_in_dim.36
  65.3 5.4 %all-to-all-start.5 = ((f32[64,3,512]{2,1,0:T(4,128)}), f32[64,3,512]{2,1,0:T(4,128)S(1)}, u32[]{:S(2)}, u32[]{:S(2)}) async-start(f32[64,3,512]{2,1,0:T(4,128)} %broadcast_in_dim.36), calls=%async_computation.7 | async-start | bytes 1048576 | tf_op jit(solution)/shard_map/all_to_all | solution.py:14
  70.7 0.0 reduce-scatter.3.cloned.1.call-start
  70.8 106.1 %all-gather.2.cloned.1.call-done = bf16[8192,512]{1,0:T(8,128)(2,1)} async-done(((bf16[128,512]{1,0:T(8,128)(2,1)}), bf16[8192,512]{1,0:T(8,128)(2,1)}) %all-gather.2.cloned.1.call-update) | async-done | bytes 8388624 | tf_op jit(solution)/shard_map/all_gather | solution.py:77
  176.9 6.2 %convolution_multiply_fusion = f32[8192,64]{0,1:T(8,128)S(1)} fusion(bf16[8192,512]{1,0:T(8,128)(2,1)} %all-gather.2.cloned.1.call-done, f32[8192]{0:T(1024)S(1)} %get-tuple-element.11, bf16[64,3,512]{2,0,1:T(8,128)(2,1)} %param.10), kind=kOutput, calls=%fused_computation | convolution fusion | flops 537395200 | bytes 10584064 | tf_op jit(solution)/shard_map/dot_general | solution.py:92
  183.1 2.6 convolution_multiply_fusion.1
  185.7 2.6 fusion.1
  188.3 2.7 copy.46
  191.0 4.5 %copy.47 = f32[2,4,64,1,16,64]{5,4,2,0,1,3:T(8,128)} copy(f32[2,4,64,1,16,64]{5,4,1,0,2,3:T(8,128)} %bitcast.80) | data formatting | bytes 4194304 | tf_op jit(solution)/shard_map/reshape | solution.py:35
  195.6 0.0 reduce-scatter.3.cloned.1.call-update
  195.6 1.2 copy-done.2
  196.8 1.3 copy.52
  198.1 9.1 %all-to-all-start.4 = ((bf16[128,64,64]{0,2,1:T(8,128)(2,1)}), bf16[128,64,64]{0,2,1:T(8,128)(2,1)S(1)}, u32[]{:S(2)}, u32[]{:S(2)}) async-start(bf16[128,64,64]{0,2,1:T(8,128)(2,1)} %bitcast.19), calls=%async_computation.6 | async-start | bytes 2097152 | tf_op jit(solution)/shard_map/all_to_all | solution.py:75
  207.2 0.0 reduce-scatter.5.cloned.1.call-start
  207.2 40.2 %reduce-scatter.3.cloned.1.call-done = f32[2,64,1,16,64]{4,3,1,0,2:T(8,128)} async-done(((f32[8,64,1,16,64]{4,3,1,0,2:T(8,128)}), f32[2,64,1,16,64]{4,3,1,0,2:T(8,128)}) %reduce-scatter.3.cloned.1.call-update) | async-done | bytes 524304 | tf_op jit(solution)/shard_map/reduce_scatter | solution.py:39
  247.5 0.0 reduce-scatter.5.cloned.1.call-update
  247.5 0.7 reduce_sum.39
  248.2 8.6 %all-to-all-done.4 = bf16[128,64,64]{0,2,1:T(8,128)(2,1)S(1)} async-done(((bf16[128,64,64]{0,2,1:T(8,128)(2,1)}), bf16[128,64,64]{0,2,1:T(8,128)(2,1)S(1)}, u32[]{:S(2)}, u32[]{:S(2)}) %all-to-all-start.4) | async-done | bytes 1048608 | tf_op jit(solution)/shard_map/all_to_all | solution.py:75
  256.8 4.9 %convolution_bitcast_fusion = f32[64,1,512]{2,0,1:T(8,128)S(1)} fusion(bf16[8192,512]{1,0:T(8,128)(2,1)} %all-gather.2.cloned.1.call-done, pred[8192]{0:T(1024)(128)(4,1)S(1)} %get-tuple-element.12, bf16[128,64,64]{0,2,1:T(8,128)(2,1)S(1)} %all-to-all-done.4), kind=kOutput, calls=%fused_computation.6 | convolution fusion | flops 537395200 | bytes 9576448 | tf_op jit(solution)/shard_map/dot_general | solution.py:101
  261.7 53.3 %reduce-scatter.5.cloned.1.call-done = f32[1,64,1,16,64]{4,3,1,0,2:T(8,128)} async-done(((f32[2,64,1,16,64]{4,3,1,0,2:T(8,128)}), f32[1,64,1,16,64]{4,3,1,0,2:T(8,128)}) %reduce-scatter.5.cloned.1.call-update) | async-done | bytes 262160 | tf_op jit(solution)/shard_map/reduce_scatter | solution.py:39
  315.1 1.1 convert_bitcast_fusion
  316.2 0.9 reshape.100
  317.0 15.1 %all-to-all-start.2 = ((bf16[64,2,512]{2,1,0:T(2,128)(2,1)}), bf16[64,2,512]{2,1,0:T(2,128)(2,1)S(1)}, u32[]{:S(2)}, u32[]{:S(2)}) async-start(bf16[64,2,512]{2,1,0:T(2,128)(2,1)} %reshape.100), calls=%async_computation.4 | async-start | bytes 262144 | tf_op jit(solution)/shard_map/all_to_all | solution.py:115
  332.1 4.9 %convolution_bitcast_fusion.1 = f32[64,1,512]{2,0,1:T(8,128)S(1)} fusion(bf16[8192,512]{1,0:T(8,128)(2,1)} %all-gather.2.cloned.1.call-done, pred[8192]{0:T(1024)(128)(4,1)S(1)} %get-tuple-element.14, bf16[128,64,64]{0,2,1:T(8,128)(2,1)S(1)} %all-to-all-done.4), kind=kOutput, calls=%fused_computation.7 | convolution fusion | flops 537395200 | bytes 9576448 | tf_op jit(solution)/shard_map/dot_general | solution.py:101
  337.0 8.7 %all-to-all-done.2 = bf16[64,2,512]{2,1,0:T(2,128)(2,1)S(1)} async-done(((bf16[64,2,512]{2,1,0:T(2,128)(2,1)}), bf16[64,2,512]{2,1,0:T(2,128)(2,1)S(1)}, u32[]{:S(2)}, u32[]{:S(2)}) %all-to-all-start.2) | async-done | bytes 131104 | tf_op jit(solution)/shard_map/all_to_all | solution.py:115
  345.7 0.2 reshape.101
  345.9 0.1 copy.48
  346.0 0.3 all_to_all.54
  346.3 2.7 copy.49
  349.0 0.5 broadcast.70
  349.6 23.5 %reduce.1 = bf16[4096,16]{1,0:T(8,128)(2,1)} reduce(bf16[4096,1,16]{2,1,0:T(2,128)(2,1)S(1)} %bitcast.81, bf16[]{:T(256)} %broadcast.70), dimensions={1}, to_apply=%bitcast.57.reduce_sub_computation | reduce | bytes 262146
  373.0 3.1 reshape.102
  376.1 9.9 %all-to-all-start.3 = ((bf16[8,2,4096]{2,1,0:T(2,128)(2,1)}), bf16[8,2,4096]{2,1,0:T(2,128)(2,1)S(1)}, u32[]{:S(2)}, u32[]{:S(2)}) async-start(bf16[8,2,4096]{2,1,0:T(2,128)(2,1)} %reshape.102), calls=%async_computation.5 | async-start | bytes 262144 | tf_op jit(solution)/shard_map/all_to_all | solution.py:116
  386.0 4.9 %convolution_bitcast_fusion.2 = f32[64,1,512]{2,0,1:T(8,128)S(1)} fusion(bf16[8192,512]{1,0:T(8,128)(2,1)} %all-gather.2.cloned.1.call-done, pred[8192]{0:T(1024)(128)(4,1)S(1)} %get-tuple-element.6, bf16[128,64,64]{0,2,1:T(8,128)(2,1)S(1)} %all-to-all-done.4), kind=kOutput, calls=%fused_computation.8 | convolution fusion | flops 537395200 | bytes 9576448 | tf_op jit(solution)/shard_map/dot_general | solution.py:101
  390.9 0.8 pad_maximum_fusion
  391.7 12.6 %all-to-all-done.3 = bf16[8,2,4096]{2,1,0:T(2,128)(2,1)S(1)} async-done(((bf16[8,2,4096]{2,1,0:T(2,128)(2,1)}), bf16[8,2,4096]{2,1,0:T(2,128)(2,1)S(1)}, u32[]{:S(2)}, u32[]{:S(2)}) %all-to-all-start.3) | async-done | bytes 131104 | tf_op jit(solution)/shard_map/all_to_all | solution.py:116
  404.3 1.8 reshape.103
  406.1 2.0 copy.50
  408.1 0.7 copy.51
  (15 shorter events, 0.2 us)
Async XLA Ops:
  7.2 0.7 copy-start
  7.2 169.7 %all-gather.2.cloned.1.call-start = ((), (), s32[]{:S(2)}) async-start(), calls=%async_computation.8 | async-start | bytes 8519680 | tf_op jit(solution)/shard_map/all_gather | solution.py:77
  43.9 20.5 %all-to-all-start = ((s32[64,1,128]{2,1,0:T(1,128)}), s32[64,1,128]{2,1,0:T(1,128)S(1)}, u32[]{:S(2)}, u32[]{:S(2)}) async-start(s32[64,1,128]{2,1,0:T(1,128)} %stack.10), calls=%async_computation | async-start | bytes 65536 | tf_op jit(solution)/shard_map/all_to_all | solution.py:79
  65.3 132.8 %all-to-all-start.5 = ((f32[64,3,512]{2,1,0:T(4,128)}), f32[64,3,512]{2,1,0:T(4,128)S(1)}, u32[]{:S(2)}, u32[]{:S(2)}) async-start(f32[64,3,512]{2,1,0:T(4,128)} %broadcast_in_dim.36), calls=%async_computation.7 | async-start | bytes 1048576 | tf_op jit(solution)/shard_map/all_to_all | solution.py:14
  70.7 176.7 %reduce-scatter.3.cloned.1.call-start = ((), (), s32[]{:S(2)}) async-start(), calls=%async_computation.9 | async-start | bytes 5242880 | tf_op jit(solution)/shard_map/reduce_scatter | solution.py:39
  176.9 6.2 %copy-start.1 = (bf16[8192,512]{1,0:T(8,128)(2,1)S(1)}, bf16[8192,512]{1,0:T(8,128)(2,1)}, u32[]{:S(2)}) copy-start(bf16[8192,512]{1,0:T(8,128)(2,1)} %all-gather.2.cloned.1.call-done) | copy-start | bytes 25165828
  176.9 6.2 %copy-start.3 = (bf16[64,3,512]{2,0,1:T(8,128)(2,1)S(1)}, bf16[64,3,512]{2,0,1:T(8,128)(2,1)}, u32[]{:S(2)}) copy-start(bf16[64,3,512]{2,0,1:T(8,128)(2,1)} %param.10) | copy-start | bytes 589828
  195.6 1.2 copy-start.2
  198.1 58.7 %all-to-all-start.4 = ((bf16[128,64,64]{0,2,1:T(8,128)(2,1)}), bf16[128,64,64]{0,2,1:T(8,128)(2,1)S(1)}, u32[]{:S(2)}, u32[]{:S(2)}) async-start(bf16[128,64,64]{0,2,1:T(8,128)(2,1)} %bitcast.19), calls=%async_computation.6 | async-start | bytes 2097152 | tf_op jit(solution)/shard_map/all_to_all | solution.py:75
  207.2 107.9 %reduce-scatter.5.cloned.1.call-start = ((), (), s32[]{:S(2)}) async-start(), calls=%async_computation.10 | async-start | bytes 1572864 | tf_op jit(solution)/shard_map/reduce_scatter | solution.py:39
  317.0 28.7 %all-to-all-start.2 = ((bf16[64,2,512]{2,1,0:T(2,128)(2,1)}), bf16[64,2,512]{2,1,0:T(2,128)(2,1)S(1)}, u32[]{:S(2)}, u32[]{:S(2)}) async-start(bf16[64,2,512]{2,1,0:T(2,128)(2,1)} %reshape.100), calls=%async_computation.4 | async-start | bytes 262144 | tf_op jit(solution)/shard_map/all_to_all | solution.py:115
  376.1 28.2 %all-to-all-start.3 = ((bf16[8,2,4096]{2,1,0:T(2,128)(2,1)}), bf16[8,2,4096]{2,1,0:T(2,128)(2,1)S(1)}, u32[]{:S(2)}, u32[]{:S(2)}) async-start(bf16[8,2,4096]{2,1,0:T(2,128)(2,1)} %reshape.102), calls=%async_computation.5 | async-start | bytes 262144 | tf_op jit(solution)/shard_map/all_to_all | solution.py:116
Sparse Core Ops, SparseCore 0:
  42.7 134.1 all-gather.1
  195.7 51.6 reduce-scatter.2
  250.3 64.7 reduce-scatter.4
